TPU v7x, 256 devices: a whole 4x4x8 slice. The times are simulated.
256 devices in a mesh: path: 32 (over y, x, core), fac: 8 (over z).
Axes of the slice: x: 4, y: 4, z: 8, core: 2. Of those that a mesh axis runs over, the one named last changes fastest.
Arguments:
- shocks: bfloat16 [4, 2048, 8192], P(None, 'path', 'fac'), may hold values from -6 to 6
- chol_factor: bfloat16 [8192, 8192], P('path', 'fac')
- factor_vol: float32 [8192], P('fac'), may hold values from 0.3 to 1.5
- trade_loading: bfloat16 [8192, 4096], P(None, 'fac'), may hold values from -0.0625 to 0.0625
- basis_loading: bfloat16 [8192, 64], replicated, may hold values from -0.0625 to 0.0625
- trade_set: int32 [4096], P('fac'), may hold values from 0 to 4095, as said below
Outputs:
- exposure: float32 [4, 2048, 4096], P(None, 'path', 'fac')
Inputs may be any that keep to these rules, and one draw needn't show every extreme that they name: Each trade belongs to a netting set of its own block: trade_set[k] // 512 equals k // 512.
All inputs are finite; a program needn't handle non-finite values.
Results may differ from a plain program's by a relative error of at most 0.0047.
Values may be sent and summed in bfloat16 or wider, within the bound.
A program may use at most 128 MiB of HBM per device.

v0:
```python
import math
import jax
import jax.numpy as jnp
from jax import lax
from jax.sharding import PartitionSpec as P

F = 8192
NSETS = 4096


def solve_step(gram, moment, basis, total_paths):
    ridged = gram + 0.01 * total_paths * jnp.eye(gram.shape[0], dtype=jnp.float32)
    factor = jnp.linalg.cholesky(ridged)
    coef = jax.scipy.linalg.cho_solve((factor, True), moment)
    predicted = jnp.dot(
        basis, coef, precision=lax.Precision.HIGHEST, preferred_element_type=jnp.float32
    )
    return jnp.maximum(predicted, 0.0)


def on_device(shocks, chol_factor, factor_vol, trade_loading, basis_loading, trade_set):
    step_count, path_count, fac_width = shocks.shape
    row_count = step_count * path_count
    flat_shocks = shocks.reshape(row_count, fac_width)
    factor_share = F // lax.axis_size("fac")
    contract_last = (((1,), (1,)), ((), ()))
    full_rows = lax.all_gather(chol_factor, "path", axis=0, tiled=True)
    increments = lax.psum_scatter(
        lax.dot_general(full_rows, flat_shocks, contract_last, preferred_element_type=jnp.float32),
        "fac",
        scatter_dimension=0,
        tiled=True,
    )
    scaled = increments.reshape(factor_share, step_count, path_count) * (
        factor_vol[:, None, None] / math.sqrt(step_count)
    )
    levels = jnp.cumsum(scaled, axis=1).astype(jnp.bfloat16).reshape(factor_share, row_count)
    basis_count = basis_loading.shape[1]
    contract_first = (((0,), (0,)), ((), ()))
    piece = lax.all_gather(levels, "fac", axis=0, tiled=True)
    trade_sum = lax.dot_general(
        piece, trade_loading, contract_first, preferred_element_type=jnp.float32
    )
    basis_sum = lax.dot_general(
        piece, basis_loading, contract_first, preferred_element_type=jnp.float32
    )
    values = jax.nn.softplus(trade_sum) - 1.0
    sets_here = NSETS // lax.axis_size("fac")
    local_set = trade_set % sets_here
    member = (local_set[:, None] == jnp.arange(sets_here, dtype=jnp.int32)[None, :]).astype(
        jnp.float32
    )
    netting = jnp.dot(
        values, member, precision=lax.Precision.HIGHEST, preferred_element_type=jnp.float32
    )
    basis = jnp.tanh(basis_sum).reshape(step_count, path_count, basis_count)
    netting = netting.reshape(step_count, path_count, sets_here)
    gram = jnp.einsum(
        "tpm,tpn->tmn",
        basis,
        basis,
        precision=lax.Precision.HIGHEST,
        preferred_element_type=jnp.float32,
    )
    moment = jnp.einsum(
        "tpm,tpn->tmn",
        basis,
        netting,
        precision=lax.Precision.HIGHEST,
        preferred_element_type=jnp.float32,
    )
    total_paths = path_count * lax.axis_size("path")
    results = []
    for step in range(step_count):
        gram_total, moment_total = lax.psum((gram[step], moment[step]), "path")
        results.append(solve_step(gram_total, moment_total, basis[step], total_paths))
    return jnp.stack(results)


def solution(mesh):
    in_specs = (P(None, "path", "fac"), P("path", "fac"), P("fac"), P(None, "fac"), P(), P("fac"))
    out_specs = P(None, "path", "fac")
    return jax.shard_map(
        on_device, mesh=mesh, in_specs=in_specs, out_specs=out_specs, check_vma=False
    )
```

profile of v0, /device:TPU:6, one launch (start us, length us, event | category | flops | bytes accessed | tf_op | source)
XLA Modules:
  0.0 512.1 jit_solution(6052345440305277966)
XLA Ops:
  6.5 0.7 all-gather.3.cloned.1.call-update
  7.3 83.1 %all-gather.3.cloned.1.call-done = bf16[8192,1024]{1,0:T(8,128)(2,1)} async-done(((bf16[256,1024]{1,0:T(8,128)(2,1)}), bf16[8192,1024]{1,0:T(8,128)(2,1)}) %all-gather.3.cloned.1.call-update) | async-done | bytes 16777232 | tf_op jit(solution)/shard_map/all_gather | solution.py:27
  90.4 13.6 %fusion.53 = f32[8192,256]{1,0:T(8,128)} fusion(bf16[8192,1024]{1,0:T(8,128)(2,1)} %all-gather.3.cloned.1.call-done, bf16[256,1024]{1,0:T(8,128)(2,1)} %bitcast.96), kind=kOutput, calls=%fused_computation.96 | convolution fusion | flops 4294967296 | bytes 25690112 | tf_op jit(solution)/shard_map/dot_general | solution.py:29
  104.7 94.0 %reduce-scatter.2.cloned.1.call-done = f32[1024,256]{1,0:T(8,128)} async-done(((f32[8192,256]{1,0:T(8,128)}), f32[1024,256]{1,0:T(8,128)}) %reduce-scatter.2.cloned.1.call-update) | async-done | bytes 1048592 | tf_op jit(solution)/shard_map/reduce_scatter | solution.py:28
  198.6 1.6 copy.18
  200.2 0.9 reduce-window_convert_fusion
  201.2 53.5 %all-gather.5.cloned.1.call-done = bf16[8192,256]{0,1:T(8,128)(2,1)} async-done(((bf16[1024,256]{0,1:T(8,128)(2,1)}), bf16[8192,256]{0,1:T(8,128)(2,1)}) %all-gather.5.cloned.1.call-update) | async-done | bytes 4194320 | tf_op jit(solution)/shard_map/all_gather | solution.py:40
  254.7 3.6 convolution_tanh_fusion
  258.7 7.0 %fusion.54 = f32[256,512]{1,0:T(8,128)S(1)} fusion(bf16[8192,256]{0,1:T(8,128)(2,1)} %all-gather.5.cloned.1.call-done, bf16[8192,512]{1,0:T(8,128)(2,1)} %param.12), kind=kOutput, calls=%fused_computation.97 | convolution fusion | flops 2147483648 | bytes 13107200 | tf_op jit(solution)/shard_map/dot_general | solution.py:41
  265.7 1.0 fusion.5
  268.2 0.8 slice_bitcast_fusion.3
  269.0 110.1 %all-reduce.5.cloned.1.call-done = (f32[64,64]{0,1:T(8,128)}, f32[64,64]{0,1:T(8,128)}, f32[64,64]{0,1:T(8,128)}, f32[64,64]{0,1:T(8,128)}) async-done(((f32[64,64]{0,1:T(8,128)}, f32[64,64]{0,1:T(8,128)}, f32[64,64]{0,1:T(8,128)}, f32[64,64]{0,1:T(8,128)}), (f32[64,64]{0,1:T(8,128)}, f32[64,64]{0,1:T(8,128)}, f32[64,64]{0,1:T(8,128)}, f32[64,64]{0,1:T(8,128)})) %all-reduce.5.cloned.1.call-update) | async-done | bytes 65552 | tf_op jit(solution)/shard_map/psum | solution.py:75
  379.1 0.8 select_add_fusion
  380.0 0.8 fusion.34
  380.8 5.8 %cholesky.107 = f32[64,64]{1,0:T(8,128)S(1)} custom-call(f32[64,64]{1,0:T(8,128)S(1)} %fusion.34), custom_call_target="Cholesky" | custom-call | tf_op jit(solution)/shard_map/jit(cholesky)/cholesky | solution.py:13
  387.9 0.8 fusion.39
  388.7 5.8 %cholesky.96 = f32[64,64]{1,0:T(8,128)S(1)} custom-call(f32[64,64]{1,0:T(8,128)S(1)} %fusion.39), custom_call_target="Cholesky" | custom-call | tf_op jit(solution)/shard_map/jit(cholesky)/cholesky | solution.py:13
  396.0 0.8 select_add_fusion.2
  396.9 0.8 fusion.44
  397.7 5.8 %cholesky.85 = f32[64,64]{1,0:T(8,128)S(1)} custom-call(f32[64,64]{1,0:T(8,128)S(1)} %fusion.44), custom_call_target="Cholesky" | custom-call | tf_op jit(solution)/shard_map/jit(cholesky)/cholesky | solution.py:13
  404.9 0.8 fusion.49
  405.7 5.8 %cholesky.74 = f32[64,64]{1,0:T(8,128)S(1)} custom-call(f32[64,64]{1,0:T(8,128)S(1)} %fusion.49), custom_call_target="Cholesky" | custom-call | tf_op jit(solution)/shard_map/jit(cholesky)/cholesky | solution.py:13
  412.3 4.9 custom-call.13
  417.2 4.9 custom-call.12
  422.1 4.9 custom-call.11
  427.6 4.9 custom-call.10
  432.5 64.7 %all-reduce.7.cloned.1.call-done = (f32[64,512]{1,0:T(8,128)}, f32[64,512]{1,0:T(8,128)}, f32[64,512]{1,0:T(8,128)}, f32[64,512]{1,0:T(8,128)}) async-done(((f32[64,512]{1,0:T(8,128)}, f32[64,512]{1,0:T(8,128)}, f32[64,512]{1,0:T(8,128)}, f32[64,512]{1,0:T(8,128)}), (f32[64,512]{1,0:T(8,128)}, f32[64,512]{1,0:T(8,128)}, f32[64,512]{1,0:T(8,128)}, f32[64,512]{1,0:T(8,128)})) %all-reduce.7.cloned.1.call-update) | async-done | bytes 524304 | tf_op jit(solution)/shard_map/psum | solution.py:75
  497.3 1.2 fusion.32
  499.2 1.2 fusion.37
  501.0 1.2 fusion.42
  502.9 1.2 fusion.47
  504.7 0.8 pad_maximum_fusion
  (45 shorter events, 10.8 us)
Async XLA Ops:
  6.5 248.1 %copy-start = (bf16[8192,64]{0,1:T(8,128)(2,1)S(1)}, bf16[8192,64]{0,1:T(8,128)(2,1)}, u32[]{:S(2)}) copy-start(bf16[8192,64]{0,1:T(8,128)(2,1)} %param.13) | copy-start | bytes 3145732
  6.5 83.8 %all-gather.3.cloned.1.call-start = ((), (), s32[]{:S(2)}) async-start(), calls=%async_computation.1 | async-start | bytes 17301504 | tf_op jit(solution)/shard_map/all_gather | solution.py:27
  7.3 191.4 %reduce-scatter.2.cloned.1.call-start = ((), (), s32[]{:S(2)}) async-start(), calls=%async_computation.2 | async-start | bytes 9437184 | tf_op jit(solution)/shard_map/reduce_scatter | solution.py:28
  104.0 0.7 copy-start.1
  104.0 97.2 %copy-start.2 = (s32[512]{0:T(512)S(1)}, s32[512]{0:T(512)}, u32[]{:S(2)}) copy-start(s32[512]{0:T(512)} %param.14) | copy-start | bytes 6148
  104.0 150.7 %all-gather.5.cloned.1.call-start = ((), (), s32[]{:S(2)}) async-start(), calls=%async_computation.3 | async-start | bytes 4718592 | tf_op jit(solution)/shard_map/all_gather | solution.py:40
  201.1 178.0 %all-reduce.5.cloned.1.call-start = ((), (), s32[]{:S(2)}) async-start(), calls=%async_computation.4 | async-start | bytes 262144 | tf_op jit(solution)/shard_map/psum | solution.py:75
  268.0 229.3 %all-reduce.7.cloned.1.call-start = ((), (), s32[]{:S(2)}) async-start(), calls=%async_computation.5 | async-start | bytes 1048576 | tf_op jit(solution)/shard_map/psum | solution.py:75
Sparse Core Ops, SparseCore 0:
  9.9 80.4 all-gather.2
  104.1 94.4 reduce-scatter.1
  201.2 53.3 all-gather.4
  268.1 111.0 all-reduce.4
  382.4 114.8 all-reduce.6
where the time goes:
time: 513 us; the launch traced here: 512 us
  waiting for transfers between devices  406 us (79%)
  other arithmetic  54.8 us (11%)
  matrix products  33.4 us (7%)
  between operations  13.4 us (3%)
    psum x2, waiting for transfers between devices, on_device(): gram_total, moment_total = lax.psum((gram[step], moment[step]), 'path')  175 us
    reduce_scatter x1, waiting for transfers between devices, on_device(): lax.psum_scatter(lax.dot_general(full_rows, flat_shocks, contract_last, p...  94 us
    all_gather x1, waiting for transfers between devices, on_device(): full_rows = lax.all_gather(chol_factor, 'path', axis=0, tiled=True)  83.1 us
    all_gather x1, waiting for transfers between devices, on_device(): piece = lax.all_gather(levels, 'fac', axis=0, tiled=True)  53.5 us
    another operation x12, other arithmetic, solve_step(): factor = jnp.linalg.cholesky(ridged)  26.2 us
    another operation x8, other arithmetic, solve_step(): coef = jax.scipy.linalg.cho_solve((factor, True), moment)  22.1 us
    dot_general x1, matrix products, on_device(): lax.dot_general(full_rows, flat_shocks, contract_last, preferred_element_...  13.6 us
  transfers between devices with their start and end apart: 5, of which 5 were waited for; matrix products, arithmetic and copies ran while one was open for 11% of the time, Pallas kernels for 0%

commit v1 on v0

--- a/solution.py
+++ b/solution.py
@@ -24,7 +24,15 @@
     flat_shocks = shocks.reshape(row_count, fac_width)
     factor_share = F // lax.axis_size("fac")
     contract_last = (((1,), (1,)), ((), ()))
-    full_rows = lax.all_gather(chol_factor, "path", axis=0, tiled=True)
+    full_rows = jnp.concatenate(
+        lax.all_to_all(
+            jnp.stack([chol_factor for _ in range(lax.axis_size("path"))], axis=0),
+            axis_name="path",
+            split_axis=0,
+            concat_axis=0,
+        ),
+        0,
+    )
     increments = lax.psum_scatter(
         lax.dot_general(full_rows, flat_shocks, contract_last, preferred_element_type=jnp.float32),
         "fac",

time: 513 us -> 619 us (1.21)
  blocking collectives: 0 us -> 191 us
  waiting for transfers between devices: 406 us -> 324 us
  matrix products: 33.4 us -> 26.5 us
    all_to_all x0 -> x1, blocking collectives: none -> 191 us  [on_device(): lax.all_to_all(jnp.stack([chol_factor for _ in range(lax.axis_size('path'...]
    all_gather x1 -> x0, waiting for transfers between devices: 83.1 us -> none  [on_device(): full_rows = lax.all_gather(chol_factor, 'path', axis=0, tiled=True)]
    dot_general x1, matrix products: 13.6 us -> 6.75 us  [on_device(): lax.dot_general(full_rows, flat_shocks, contract_last, preferred_element_...]
  transfers between devices with their start and end apart: 5 -> 4, of which waited for: 5 -> 4; matrix products, arithmetic and copies ran while one was open for 11% -> 9% of each run, Pallas kernels for 0% -> 0%
where the time goes in v1:
time: 619 us; the launch traced here: 618 us
  waiting for transfers between devices  324 us (52%)
  blocking collectives  191 us (31%)
  other arithmetic  54.8 us (9%)
  matrix products  26.5 us (4%)
  between operations  13.4 us (2%)
  local copies, waits for them, and re-layouts  7.75 us (1%)
    all_to_all x1, blocking collectives, on_device(): lax.all_to_all(jnp.stack([chol_factor for _ in range(lax.axis_size('path'...  191 us
    psum x2, waiting for transfers between devices, on_device(): gram_total, moment_total = lax.psum((gram[step], moment[step]), 'path')  175 us
    reduce_scatter x1, waiting for transfers between devices, on_device(): lax.psum_scatter(lax.dot_general(full_rows, flat_shocks, contract_last, p...  96 us
    all_gather x1, waiting for transfers between devices, on_device(): piece = lax.all_gather(levels, 'fac', axis=0, tiled=True)  53.5 us
    another operation x12, other arithmetic, solve_step(): factor = jnp.linalg.cholesky(ridged)  26.2 us
    another operation x8, other arithmetic, solve_step(): coef = jax.scipy.linalg.cho_solve((factor, True), moment)  22.1 us
  transfers between devices with their start and end apart: 4, of which 4 were waited for; matrix products, arithmetic and copies ran while one was open for 9% of the time, Pallas kernels for 0%

profile of v1, /device:TPU:6, one launch (start us, length us, event | category | flops | bytes accessed | tf_op | source)
XLA Modules:
  0.0 617.7 jit_solution(14749212158695448129)
XLA Ops:
  6.5 3.7 stack.12
  10.3 190.6 %all_to_all.5 = bf16[32,256,1024]{2,1,0:T(8,128)(2,1)S(1)} all-to-all(bf16[32,256,1024]{2,1,0:T(8,128)(2,1)S(1)} %stack.12), channel_id=1, replica_groups=mesh['path'=32,'fac'=8] {'path'}, dimensions={0} | all-to-all | bytes 33554432 | tf_op jit(solution)/shard_map/all_to_all | solution.py:28
  200.9 6.7 %fusion.53 = f32[8192,256]{1,0:T(8,128)} fusion(bf16[8192,1024]{1,0:T(8,128)(2,1)S(1)} %bitcast.94, bf16[256,1024]{1,0:T(8,128)(2,1)S(1)} %bitcast.98), kind=kOutput, calls=%fused_computation.96 | convolution fusion | flops 4294967296 | bytes 25690112 | tf_op jit(solution)/shard_map/dot_general | solution.py:37
  208.4 96.0 %reduce-scatter.2.cloned.1.call-done = f32[1024,256]{1,0:T(8,128)} async-done(((f32[8192,256]{1,0:T(8,128)}), f32[1024,256]{1,0:T(8,128)}) %reduce-scatter.2.cloned.1.call-update) | async-done | bytes 1048592 | tf_op jit(solution)/shard_map/reduce_scatter | solution.py:36
  304.4 1.6 copy.18
  306.0 0.9 reduce-window_convert_fusion
  306.9 53.5 %all-gather.2.cloned.1.call-done = bf16[8192,256]{0,1:T(8,128)(2,1)} async-done(((bf16[1024,256]{0,1:T(8,128)(2,1)}), bf16[8192,256]{0,1:T(8,128)(2,1)}) %all-gather.2.cloned.1.call-update) | async-done | bytes 4194320 | tf_op jit(solution)/shard_map/all_gather | solution.py:48
  360.4 3.6 convolution_tanh_fusion
  365.1 7.0 %fusion.54 = f32[256,512]{1,0:T(8,128)S(1)} fusion(bf16[8192,256]{0,1:T(8,128)(2,1)} %all-gather.2.cloned.1.call-done, bf16[8192,512]{1,0:T(8,128)(2,1)} %param.12), kind=kOutput, calls=%fused_computation.97 | convolution fusion | flops 2147483648 | bytes 13107200 | tf_op jit(solution)/shard_map/dot_general | solution.py:49
  372.1 1.0 fusion.5
  373.9 0.8 slice_bitcast_fusion.3
  374.7 110.1 %all-reduce.5.cloned.1.call-done = (f32[64,64]{0,1:T(8,128)}, f32[64,64]{0,1:T(8,128)}, f32[64,64]{0,1:T(8,128)}, f32[64,64]{0,1:T(8,128)}) async-done(((f32[64,64]{0,1:T(8,128)}, f32[64,64]{0,1:T(8,128)}, f32[64,64]{0,1:T(8,128)}, f32[64,64]{0,1:T(8,128)}), (f32[64,64]{0,1:T(8,128)}, f32[64,64]{0,1:T(8,128)}, f32[64,64]{0,1:T(8,128)}, f32[64,64]{0,1:T(8,128)})) %all-reduce.5.cloned.1.call-update) | async-done | bytes 65552 | tf_op jit(solution)/shard_map/psum | solution.py:83
  484.9 0.8 select_add_fusion.2
  485.7 0.8 fusion.49
  486.5 5.8 cholesky.74
  493.7 0.8 fusion.44
  494.5 5.8 cholesky.85
  501.8 0.8 select_add_fusion
  502.6 0.8 fusion.39
  503.4 5.8 cholesky.96
  510.7 0.8 fusion.34
  511.5 5.8 cholesky.107
  518.0 4.9 custom-call.10
  522.9 4.9 custom-call.11
  527.8 4.9 custom-call.12
  533.4 4.9 custom-call.13
  538.3 64.6 %all-reduce.7.cloned.1.call-done = (f32[64,512]{1,0:T(8,128)}, f32[64,512]{1,0:T(8,128)}, f32[64,512]{1,0:T(8,128)}, f32[64,512]{1,0:T(8,128)}) async-done(((f32[64,512]{1,0:T(8,128)}, f32[64,512]{1,0:T(8,128)}, f32[64,512]{1,0:T(8,128)}, f32[64,512]{1,0:T(8,128)}), (f32[64,512]{1,0:T(8,128)}, f32[64,512]{1,0:T(8,128)}, f32[64,512]{1,0:T(8,128)}, f32[64,512]{1,0:T(8,128)})) %all-reduce.7.cloned.1.call-update) | async-done | bytes 524304 | tf_op jit(solution)/shard_map/psum | solution.py:83
  602.9 1.2 fusion.47
  604.7 1.2 fusion.42
  606.6 1.2 fusion.37
  608.5 1.2 fusion.32
  610.4 0.8 pad_maximum_fusion
  (46 shorter events, 10.8 us)
Async XLA Ops:
  6.5 353.9 %copy-start = (bf16[8192,64]{0,1:T(8,128)(2,1)S(1)}, bf16[8192,64]{0,1:T(8,128)(2,1)}, u32[]{:S(2)}) copy-start(bf16[8192,64]{0,1:T(8,128)(2,1)} %param.13) | copy-start | bytes 3145732
  6.5 297.9 %reduce-scatter.2.cloned.1.call-start = ((), (), s32[]{:S(2)}) async-start(), calls=%async_computation.2 | async-start | bytes 9437184 | tf_op jit(solution)/shard_map/reduce_scatter | solution.py:36
  10.3 190.6 %copy-start.3 = (bf16[4,64,1024]{2,1,0:T(8,128)(2,1)S(1)}, bf16[4,64,1024]{2,1,0:T(8,128)(2,1)}, u32[]{:S(2)}) copy-start(bf16[4,64,1024]{2,1,0:T(8,128)(2,1)} %param.9) | copy-start | bytes 1572868
  207.7 0.7 copy-start.1
  207.7 99.3 %copy-start.2 = (s32[512]{0:T(512)S(1)}, s32[512]{0:T(512)}, u32[]{:S(2)}) copy-start(s32[512]{0:T(512)} %param.14) | copy-start | bytes 6148
  207.7 152.7 %all-gather.2.cloned.1.call-start = ((), (), s32[]{:S(2)}) async-start(), calls=%async_computation.3 | async-start | bytes 4718592 | tf_op jit(solution)/shard_map/all_gather | solution.py:48
  306.9 178.0 %all-reduce.5.cloned.1.call-start = ((), (), s32[]{:S(2)}) async-start(), calls=%async_computation.4 | async-start | bytes 262144 | tf_op jit(solution)/shard_map/psum | solution.py:83
  373.7 229.2 %all-reduce.7.cloned.1.call-start = ((), (), s32[]{:S(2)}) async-start(), calls=%async_computation.5 | async-start | bytes 1048576 | tf_op jit(solution)/shard_map/psum | solution.py:83
Sparse Core Ops, SparseCore 0:
  207.8 96.5 reduce-scatter.1
  307.0 53.3 all-gather.1
  373.8 111.0 all-reduce.4
  488.1 114.7 all-reduce.6
